TPU v7x, 768 devices: a whole 4x8x12 slice. The times are simulated.
768 devices in a mesh: row: 192 (over z, y, core), col: 4 (over x).
Axes of the slice: x: 4, y: 8, z: 12, core: 2. Of those that a mesh axis runs over, the one named last changes fastest.
Arguments:
- amplitudes: bfloat16 [24576, 128], P(('row', 'col')), may hold values from -6 to 6
- driver: bfloat16 [24576, 128], P(('row', 'col')), may hold values from -6 to 6
- ladder_integrals: bfloat16 [4, 6144, 6144], P('col', 'row'), as said below
- cycle_kernel: bfloat16 [192, 4, 64, 12288], P('row', 'col'), may hold values from -0.0546875 to 0.0546875
- cycle_target: int32 [24576], P(('row', 'col')), may hold values from 0 to 63, as said below
- vir_energy: float32 [24576], P(('row', 'col')), may hold values from 1 to 4
- occ_energy: float32 [128], replicated, may hold values from -2 to -0.5
Outputs:
- update: float32 [24576, 128], P(('row', 'col'))
Inputs may be any that keep to these rules, and one draw needn't show every extreme that they name: ladder_integrals[c] is a symmetric matrix for every c. `cycle_target`: within the 32 pairs of one tile the values are distinct; value // 16 is an owner among the tiles of the same first index and value % 16 a slot. Every tile sends exactly 16 pairs to one owner, the same owner for all tiles of one first index; the rest go to the other owners.
All inputs are finite; a program needn't handle non-finite values.
Results may differ from a plain program's by a relative error of at most 0.00084.
Values may be sent and summed in bfloat16 or wider, within the bound.
A program may use at most 32 MiB of HBM per device.

v0:
```python
import jax
import jax.numpy as jnp
from jax import lax
from jax.sharding import Mesh
from jax.sharding import PartitionSpec as P

ROW = ("row_0", "row_1", "row_2")
ROW_COL = ("row_0", "row_1", "row_2", "col")


def laid_out(parts, dim):
    parts = jnp.moveaxis(parts, 0, dim)
    shape = parts.shape
    return parts.reshape(*shape[:dim], shape[dim] * shape[dim + 1], *shape[dim + 2 :])


def stacked_from(shard, axes, sequence):
    parts = shard[None]
    for k in sequence:
        parts = lax.all_gather(parts, axes[k], axis=0, tiled=True)
    block = [lax.axis_size(axes[k]) for k in reversed(sequence)]
    parts = parts.reshape(*block, *shard.shape)
    turned = sorted(range(len(sequence)), key=lambda place: sequence[len(sequence) - 1 - place])
    return parts.transpose(*turned, *range(len(sequence), parts.ndim)).reshape(-1, *shard.shape)


def whole_of(shard, axes, sequence, dim):
    return laid_out(stacked_from(shard, axes, sequence), dim)


def body(amplitudes, driver, ladder_integrals, cycle_kernel, cycle_target, vir_energy, occ_energy):
    pair_dev, occ_width = amplitudes.shape
    ladder_tile = ladder_integrals[0]
    kernel = cycle_kernel[0, 0]
    cycle_rows = kernel.shape[0]
    col_count = lax.axis_size("col")
    capacity = cycle_rows // col_count
    cols_block = ladder_tile
    ladder = jnp.dot(
        cols_block, whole_of(amplitudes, ROW, (0, 1, 2), 0), preferred_element_type=jnp.float32
    )
    slot_ids = jnp.arange(cycle_rows, dtype=jnp.int32)
    onehot = (cycle_target[:, None] == slot_ids[None, :]).astype(jnp.bfloat16)
    placed = lax.dot_general(
        onehot, amplitudes, (((0,), (0,)), ((), ())), preferred_element_type=jnp.float32
    )
    placed = placed.astype(jnp.bfloat16).reshape(col_count, capacity, occ_width)
    my_index = lax.axis_index("col")
    buffers = lax.all_gather(placed[None], "col", axis=0, tiled=True)
    own_tile = lax.dynamic_index_in_dim(buffers, my_index, 1, keepdims=False)
    cols_block = kernel
    mixed = jnp.dot(
        cols_block,
        whole_of(own_tile.reshape(cycle_rows, occ_width), ROW, (1, 0, 2), 0),
        preferred_element_type=jnp.float32,
    )
    cycle_mixed = mixed.astype(jnp.bfloat16)
    everyone = lax.all_gather(cycle_mixed[None], "col", axis=0, tiled=True)
    everyone = everyone.reshape(col_count, col_count, capacity, occ_width)
    returned = lax.dynamic_index_in_dim(everyone, my_index, 1, keepdims=False)
    cycle_term = jnp.dot(
        onehot, returned.reshape(cycle_rows, occ_width), preferred_element_type=jnp.float32
    )
    denominator = vir_energy[:, None] - occ_energy[None, :]
    return (driver.astype(jnp.float32) + ladder + cycle_term) / denominator


def solution(mesh):
    finer = Mesh(
        mesh.devices.reshape(12, 8, 2, mesh.shape["col"]), ("row_0", "row_1", "row_2", "col")
    )
    in_specs = (
        P(ROW_COL, None),
        P(ROW_COL, None),
        P("col", ROW, None),
        P(ROW, "col", None, None),
        P(ROW_COL),
        P(ROW_COL),
        P(),
    )
    out_specs = P(ROW_COL, None)
    return jax.shard_map(body, mesh=finer, in_specs=in_specs, out_specs=out_specs, check_vma=False)
```

profile of v0, /device:TPU:1, one launch (start us, length us, event | category | flops | bytes accessed | tf_op | source)
XLA Modules:
  0.0 182.6 jit_solution(11799314522051460728)
XLA Ops:
  6.5 0.0 copy-start
  6.5 0.0 all-gather.8.cloned.1.call-start
  6.5 1.1 convolution_convert_fusion
  7.6 10.1 %all_gather.27 = bf16[4,4,16,128]{3,2,1,0:T(8,128)(2,1)S(1)} all-gather(bf16[1,4,16,128]{3,2,1,0:T(8,128)(2,1)S(1)} %bitcast.36), channel_id=1, replica_groups=mesh['row_0'=12,'row_1'=8,'row_2'=2,'col'=4] {'col'}, dimensions={0}, use_global_device_ids=true | all-gather | bytes 81920 | tf_op jit(solution)/shard_map/all_gather | solution.py:49
  17.8 21.8 %all_gather.28 = bf16[8,64,128]{2,1,0:T(8,128)(2,1)} all-gather(bf16[1,64,128]{2,1,0:T(8,128)(2,1)S(1)} %bitcast.35), channel_id=1, replica_groups=mesh['row_0'=12,'row_1'=8,'row_2'=2,'col'=4] {'row_1'}, dimensions={0}, use_global_device_ids=true | all-gather | bytes 147456 | tf_op jit(solution)/shard_map/all_gather | solution.py:20
  39.6 0.0 all-gather.8.cloned.1.call-update
  39.6 0.0 all-gather.6.cloned.1.call-start
  39.6 27.6 %all-gather = bf16[384,128]{1,0:T(8,128)(2,1)S(1)} all-gather(bf16[32,128]{1,0:T(8,128)(2,1)} %param.7), channel_id=2, replica_groups=mesh['row_0'=12,'row_1'=8,'row_2'=2,'col'=4] {'row_0'}, dimensions={0}, use_global_device_ids=true | all-gather | bytes 106496 | tf_op jit(solution)/shard_map/all_gather | solution.py:20
  67.3 22.3 %all_gather.25 = bf16[96,32,128]{2,1,0:T(8,128)(2,1)} all-gather(bf16[12,32,128]{2,1,0:T(8,128)(2,1)S(1)} %bitcast.33), channel_id=1, replica_groups=mesh['row_0'=12,'row_1'=8,'row_2'=2,'col'=4] {'row_1'}, dimensions={0}, use_global_device_ids=true | all-gather | bytes 884736 | tf_op jit(solution)/shard_map/all_gather | solution.py:20
  89.6 0.0 all-gather.6.cloned.1.call-update
  89.6 0.0 all-gather.10.cloned.1.call-start
  89.7 17.2 %all-gather.8.cloned.1.call-done = bf16[96,64,128]{2,1,0:T(8,128)(2,1)} async-done(((bf16[8,64,128]{2,1,0:T(8,128)(2,1)}), bf16[96,64,128]{2,1,0:T(8,128)(2,1)}) %all-gather.8.cloned.1.call-update) | async-done | bytes 1572880 | tf_op jit(solution)/shard_map/all_gather | solution.py:20
  106.9 0.0 all-gather.10.cloned.1.call-update
  106.9 29.0 %all-gather.6.cloned.1.call-done = bf16[192,32,128]{2,1,0:T(8,128)(2,1)} async-done(((bf16[96,32,128]{2,1,0:T(8,128)(2,1)}), bf16[192,32,128]{2,1,0:T(8,128)(2,1)}) %all-gather.6.cloned.1.call-update) | async-done | bytes 1572880 | tf_op jit(solution)/shard_map/all_gather | solution.py:20
  135.9 0.0 copy-start.1
  135.9 0.0 copy-start.2
  135.9 1.9 %copy.10 = bf16[12,8,2,32,128]{4,3,2,1,0:T(8,128)(2,1)S(1)} copy(bf16[12,8,2,32,128]{4,3,0,1,2:T(8,128)(2,1)} %bitcast.32) | data formatting | bytes 3145728 | tf_op jit(solution)/shard_map/transpose | solution.py:24
  137.8 0.0 copy-done.1
  137.8 0.0 copy-done.2
  137.8 0.4 convolution_add_fusion.1
  138.2 24.5 %all-gather.10.cloned.1.call-done = bf16[192,64,128]{2,1,0:T(8,128)(2,1)} async-done(((bf16[96,64,128]{2,1,0:T(8,128)(2,1)}), bf16[192,64,128]{2,1,0:T(8,128)(2,1)}) %all-gather.10.cloned.1.call-update) | async-done | bytes 3145744 | tf_op jit(solution)/shard_map/all_gather | solution.py:20
  162.7 2.9 %copy.11 = bf16[12,8,2,64,128]{4,3,2,1,0:T(8,128)(2,1)S(1)} copy(bf16[12,8,2,64,128]{4,3,1,0,2:T(8,128)(2,1)} %bitcast.31) | data formatting | bytes 6291456 | tf_op jit(solution)/shard_map/transpose | solution.py:24
  165.6 0.0 copy-done
  165.6 0.0 copy-start.3
  165.6 0.0 copy-start.4
  165.6 0.0 copy-start.5
  165.6 0.7 fusion.5
  166.3 9.0 %all-gather.1 = bf16[256,128]{1,0:T(8,128)(2,1)S(1)} all-gather(bf16[64,128]{1,0:T(8,128)(2,1)S(1)} %fusion.5), channel_id=3, replica_groups=mesh['row_0'=12,'row_1'=8,'row_2'=2,'col'=4] {'col'}, dimensions={0}, use_global_device_ids=true | all-gather | bytes 81920 | tf_op jit(solution)/shard_map/all_gather | solution.py:58
  175.3 0.0 copy-done.3
  175.3 0.0 copy-done.4
  175.3 0.0 copy-done.5
  175.3 0.8 fusion.8
  (2 shorter events, 0.0 us)
Async XLA Ops:
  6.5 159.0 %copy-start = (bf16[1,1,64,12288]{3,2,1,0:T(8,128)(2,1)S(1)}, bf16[1,1,64,12288]{3,2,1,0:T(8,128)(2,1)}, u32[]{:S(2)}) copy-start(bf16[1,1,64,12288]{3,2,1,0:T(8,128)(2,1)} %param.10) | copy-start | bytes 4718596
  6.5 100.3 %all-gather.8.cloned.1.call-start = ((), (), s32[]{:S(2)}) async-start(), calls=%async_computation.1 | async-start | bytes 1703936 | tf_op jit(solution)/shard_map/all_gather | solution.py:20
  39.6 96.3 %all-gather.6.cloned.1.call-start = ((), (), s32[]{:S(2)}) async-start(), calls=%async_computation | async-start | bytes 2359296 | tf_op jit(solution)/shard_map/all_gather | solution.py:20
  89.6 73.0 %all-gather.10.cloned.1.call-start = ((), (), s32[]{:S(2)}) async-start(), calls=%async_computation.2 | async-start | bytes 4718592 | tf_op jit(solution)/shard_map/all_gather | solution.py:20
  135.9 1.9 %copy-start.1 = (bf16[1,32,6144]{2,1,0:T(8,128)(2,1)S(1)}, bf16[1,32,6144]{2,1,0:T(8,128)(2,1)}, u32[]{:S(2)}) copy-start(bf16[1,32,6144]{2,1,0:T(8,128)(2,1)} %param.9) | copy-start | bytes 1179652
  135.9 1.9 %copy-start.2 = (bf16[32,128]{1,0:T(8,128)(2,1)S(1)}, bf16[32,128]{1,0:T(8,128)(2,1)}, u32[]{:S(2)}) copy-start(bf16[32,128]{1,0:T(8,128)(2,1)} %param.8) | copy-start | bytes 24580
  165.6 9.7 %copy-start.3 = (s32[32]{0:T(128)S(1)}, s32[32]{0:T(128)}, u32[]{:S(2)}) copy-start(s32[32]{0:T(128)} %param.11) | copy-start | bytes 388
  165.6 9.7 %copy-start.4 = (f32[128]{0:T(128)S(1)}, f32[128]{0:T(128)}, u32[]{:S(2)}) copy-start(f32[128]{0:T(128)} %param.13) | copy-start | bytes 1540
  165.6 9.7 %copy-start.5 = (f32[32]{0:T(128)S(1)}, f32[32]{0:T(128)}, u32[]{:S(2)}) copy-start(f32[32]{0:T(128)} %param.12) | copy-start | bytes 388
Sparse Core Ops, SparseCore 0:
  39.7 67.1 all-gather.7
  109.2 26.6 all-gather.5
  138.3 24.3 all-gather.9
where the time goes:
time: 183 us
  blocking collectives  90.8 us (50%)
  waiting for transfers between devices  70.7 us (39%)
  between operations  13.2 us (7%)
  local copies, waits for them, and re-layouts  4.84 us (3%)
  matrix products  2.92 us (2%)
    all_gather x3, blocking collectives, stacked_from(): parts = lax.all_gather(parts, axes[k], axis=0, tiled=True)  71.7 us
    all_gather x3, waiting for transfers between devices, stacked_from(): parts = lax.all_gather(parts, axes[k], axis=0, tiled=True)  70.7 us
    all_gather x1, blocking collectives, body(): buffers = lax.all_gather(placed[None], 'col', axis=0, tiled=True)  10.1 us
    all_gather x1, blocking collectives, body(): everyone = lax.all_gather(cycle_mixed[None], 'col', axis=0, tiled=True)  8.98 us
    transpose x2, local copies, waits for them, and re-layouts, stacked_from(): parts.transpose(*turned, *range(len(sequence), parts.ndim))  4.81 us
  transfers between devices with their start and end apart: 3, of which 3 were waited for; matrix products, arithmetic and copies ran while one was open for 1% of the time, Pallas kernels for 0%

commit v1 on v0

v1 whole, which is shorter than its diff:
```python
import functools

import jax
import jax.numpy as jnp
from jax import lax
from jax.experimental import pallas as pl
from jax.experimental.pallas import tpu as pltpu
from jax.sharding import Mesh
from jax.sharding import PartitionSpec as P

ROW = ("row_0", "row_1", "row_2")
ROW_COL = ("row_0", "row_1", "row_2", "col")
MESH = pl.DeviceIdType.MESH
CORES = 2


def fused(
    nz, ny, nx, amp_ref, tgt_ref, ladder_hbm, cycle_hbm, out_ref,
    gath, ladder_v, cycle_v, placed, mix, ret,
    w_sem, ring_send, first_recv, second_recv, part_send, part_recv,
    x_send, x_recv, back_send, back_recv,
):
    z, y, core, x = (lax.axis_index(a) for a in ROW_COL)
    pair, occ = amp_ref.shape
    cap = placed.shape[1]
    crow = nx * cap
    blocks = nz * ny

    load_l = pltpu.make_async_copy(ladder_hbm, ladder_v, w_sem.at[0])
    load_c = pltpu.make_async_copy(cycle_hbm, cycle_v, w_sem.at[1])
    load_l.start()
    load_c.start()

    def at(dz=0, dy=0, dx=0, dc=0):
        return (
            lax.rem(z + dz + nz, nz), lax.rem(y + dy + ny, ny),
            lax.rem(core + dc, CORES), lax.rem(x + dx, nx),
        )

    barrier = pltpu.get_barrier_semaphore()
    peers = [at(dz=1), at(dz=-1), at(dy=1), at(dy=-1), at(dc=1)]
    peers += [at(dx=j) for j in range(1, nx)]
    for peer in peers:
        pl.semaphore_signal(barrier, inc=1, device_id=peer, device_id_type=MESH)

    slot_ids = lax.broadcasted_iota(jnp.int32, (crow, pair), 0)
    onehot = (slot_ids == tgt_ref[...]).astype(jnp.float32).astype(jnp.bfloat16)
    own = jnp.dot(onehot, amp_ref[...], preferred_element_type=jnp.float32)
    placed[...] = own.astype(jnp.bfloat16).reshape(nx, cap, occ)

    my_slot = jnp.where(core == 0, z * ny + y, y * nz + z)
    gath[core, my_slot, pl.ds(0, pair), :] = amp_ref[...]
    my_part = pl.ds(pl.multiple_of(pair + x * cap, cap), cap)
    gath[core, my_slot, my_part, :] = placed[x]

    pl.semaphore_wait(barrier, len(peers))

    def remote(src, dst, send_sem, recv_sem, device):
        return pltpu.make_async_remote_copy(
            src_ref=src, dst_ref=dst, send_sem=send_sem, recv_sem=recv_sem,
            device_id=device, device_id_type=MESH,
        )

    def out_x(j):
        to = at(dx=j)
        return remote(
            placed.at[to[3]], gath.at[core, my_slot, my_part, :], x_send.at[j], x_recv.at[j], to
        )

    for j in range(1, nx):
        out_x(j).start()
    for j in range(1, nx):
        out_x(j).wait_recv()

    partner = at(dc=1)

    def plane(p):
        n1, n2 = (ny, nz) if p == 0 else (nz, ny)
        i1, i2 = (y, z) if p == 0 else (z, y)
        first = [at(dy=1), at(dy=-1)] if p == 0 else [at(dz=1), at(dz=-1)]
        second = [at(dz=1), at(dz=-1)] if p == 0 else [at(dy=1), at(dy=-1)]

        def block(a2, a1):
            return gath.at[p, lax.rem(a2 + 2 * n2, n2) * n1 + lax.rem(a1 + 2 * n1, n1)]

        def ring(src, recv_sem, device):
            return remote(src, src, ring_send, recv_sem, device)

        def to_partner(src):
            remote(src, src, part_send, part_recv, partner).start()

        def launch(k, src):
            for d in range(2):
                ring(src, second_recv.at[d, k * (n2 // 2)], second[d]).start()
            to_partner(src)

        def step(t, carry):
            def column(k, carry):
                s1 = (k + 1) // 2
                down = lax.rem(k + 1, 2)
                j = jnp.where(down == 0, i1 - s1, i1 + s1)

                @pl.when(t == s1)
                def _():
                    src = block(i2, j)
                    for d in range(2):

                        @pl.when((k > 0) & (down == d))
                        def _():
                            ring(src, first_recv.at[d, s1 - 1], first[d]).wait_recv()

                            @pl.when(k + 2 < n1)
                            def _():
                                ring(src, first_recv.at[d, s1], first[d]).start()

                    @pl.when(k == 0)
                    def _():
                        for d in range(2):
                            ring(src, first_recv.at[d, 0], first[d]).start()

                    launch(k, src)

                s2 = t - s1
                for d in range(2):
                    if n2 % 2 == 0:
                        last = jnp.where(down == d, n2 // 2, n2 // 2 - 1)
                    else:
                        last = n2 // 2

                    @pl.when((s2 >= 1) & (s2 <= last))
                    def _():
                        src = block(i2 - s2 if d == 0 else i2 + s2, j)
                        base = k * (n2 // 2)
                        ring(src, second_recv.at[d, base + s2 - 1], second[d]).wait_recv()

                        @pl.when(s2 < last)
                        def _():
                            ring(src, second_recv.at[d, base + s2], second[d]).start()

                        to_partner(src)

                return carry

            return lax.fori_loop(0, n1, column, carry)

        lax.fori_loop(0, n1 // 2 + n2 // 2 + 1, step, 0)

    for p in range(CORES):
        pl.when(core == p)(functools.partial(plane, p))

    whole = gath.at[1 - core]
    remote(whole, whole, part_send, part_recv, partner).wait_recv()
    load_l.wait()
    load_c.wait()

    def pieces(zz, y0, count, lo, size):
        return jnp.concatenate(
            [
                gath[c, (zz * ny + y0 + i) if c == 0 else ((y0 + i) * nz + zz), pl.ds(lo, size), :]
                for i in range(count)
                for c in range(CORES)
            ],
            axis=0,
        )

    lad_y = min(ny, 256 // (CORES * pair))
    cyc_y = min(ny, 256 // (CORES * crow))

    def contract(zz, carry):
        lad, cyc = carry
        for y0 in range(0, ny, lad_y):
            width = lad_y * CORES * pair
            start = pl.multiple_of((zz * ny + y0) * CORES * pair, width)
            lad += jnp.dot(
                ladder_v[:, pl.ds(start, width)], pieces(zz, y0, lad_y, 0, pair),
                preferred_element_type=jnp.float32,
            )
        for y0 in range(0, ny, cyc_y):
            width = cyc_y * CORES * crow
            start = pl.multiple_of((zz * ny + y0) * CORES * crow, width)
            cyc += jnp.dot(
                cycle_v[:, pl.ds(start, width)], pieces(zz, y0, cyc_y, pair, crow),
                preferred_element_type=jnp.float32,
            )
        return lad, cyc

    lad, cyc = lax.fori_loop(
        0, nz, contract,
        (jnp.zeros((pair, occ), jnp.float32), jnp.zeros((crow, occ), jnp.float32)),
    )
    mix[...] = cyc.astype(jnp.bfloat16).reshape(nx, cap, occ)
    ret[x] = mix[x]

    def back_x(j):
        to = at(dx=j)
        return remote(mix.at[to[3]], ret.at[x], back_send.at[j], back_recv.at[j], to)

    for j in range(1, nx):
        back_x(j).start()

    sent = gath.at[core, pl.ds(0, blocks - 1)]
    remote(sent, sent, ring_send, first_recv.at[0, 0], partner).wait_send()
    mine = gath.at[core]
    remote(mine, mine, part_send, part_recv, partner).wait_send()
    for j in range(1, nx):
        out_x(j).wait_send()
        back_x(j).wait_recv()
        back_x(j).wait_send()
    term = lax.dot_general(
        onehot, ret[...].reshape(crow, occ), (((0,), (0,)), ((), ())),
        preferred_element_type=jnp.float32,
    )
    out_ref[...] = lad + term


def body(nz, ny, nx, amplitudes, driver, ladder_integrals, cycle_kernel, cycle_target, vir_energy, occ_energy):
    pair, occ = amplitudes.shape
    crow = cycle_kernel.shape[2]
    cap = crow // nx
    blocks = nz * ny
    half = max((ny // 2) * nz, (nz // 2) * ny)
    vmem = pl.BlockSpec(memory_space=pltpu.VMEM)
    hbm = pl.BlockSpec(memory_space=pl.ANY)
    dma = pltpu.SemaphoreType.DMA
    total = pl.pallas_call(
        functools.partial(fused, nz, ny, nx),
        out_shape=jax.ShapeDtypeStruct((pair, occ), jnp.float32),
        in_specs=[vmem, vmem, hbm, hbm],
        out_specs=vmem,
        scratch_shapes=[
            pltpu.VMEM((CORES, blocks, pair + crow, occ), jnp.bfloat16),
            pltpu.VMEM(ladder_integrals.shape[1:], jnp.bfloat16),
            pltpu.VMEM(cycle_kernel.shape[2:], jnp.bfloat16),
            pltpu.VMEM((nx, cap, occ), jnp.bfloat16),
            pltpu.VMEM((nx, cap, occ), jnp.bfloat16),
            pltpu.VMEM((nx, cap, occ), jnp.bfloat16),
            dma((2,)),
            dma,
            dma((2, max(ny, nz) // 2)),
            dma((2, half)),
            dma,
            dma,
            dma((nx,)),
            dma((nx,)),
            dma((nx,)),
            dma((nx,)),
        ],
        compiler_params=pltpu.CompilerParams(collective_id=0, has_side_effects=True),
    )(amplitudes, cycle_target.reshape(1, pair), ladder_integrals[0], cycle_kernel[0, 0])
    denominator = vir_energy[:, None] - occ_energy[None, :]
    return (driver.astype(jnp.float32) + total) / denominator


def solution(mesh, sizes=(12, 8)):
    nz, ny = sizes
    nx = mesh.shape["col"]
    finer = Mesh(mesh.devices.reshape(nz, ny, CORES, nx), ROW_COL)
    in_specs = (
        P(ROW_COL, None),
        P(ROW_COL, None),
        P("col", ROW, None),
        P(ROW, "col", None, None),
        P(ROW_COL),
        P(ROW_COL),
        P(),
    )
    return jax.shard_map(
        functools.partial(body, nz, ny, nx), mesh=finer, in_specs=in_specs,
        out_specs=P(ROW_COL, None), check_vma=False,
    )
```

time: 183 us -> 66.9 us (0.37)
  blocking collectives: 90.8 us -> 0 us
  waiting for transfers between devices: 70.7 us -> 0 us
  Pallas kernels: 0 us -> 65.2 us
  between operations: 13.2 us -> 0.04 us
  local copies, waits for them, and re-layouts: 4.84 us -> 0.01 us
  matrix products: 2.92 us -> 0 us
    all_gather x5 -> x0, blocking collectives: 90.8 us -> none  [the longest x3 71.7 us: stacked_from(): parts = lax.all_gather(parts, axes[k], axis=0, tiled=True)]
    all_gather x3 -> x0, waiting for transfers between devices: 70.7 us -> none  [stacked_from(): parts = lax.all_gather(parts, axes[k], axis=0, tiled=True)]
    pallas_call x0 -> x1, Pallas kernels: none -> 65.2 us  [body(): pl.pallas_call(functools.partial(fused, nz, ny, nx), out_shape=jax.ShapeD...]
    transpose x2 -> x0, local copies, waits for them, and re-layouts: 4.81 us -> none  [stacked_from(): parts.transpose(*turned, *range(len(sequence), parts.ndim))]
    dot_general x4 -> x0, matrix products: 2.92 us -> none  [the longest x1 1.1 us: body(): lax.dot_general(onehot, amplitudes, (((0,), (0,)), ((), ())), preferred_e...]
  transfers between devices with their start and end apart: 3 -> 0, of which waited for: 3 -> 0; matrix products, arithmetic and copies ran while one was open for 1% -> 0% of each run, Pallas kernels for 0% -> 0%
where the time goes in v1:
time: 66.9 us; the launch traced here: 66.6 us
  Pallas kernels  65.2 us (97%)
  other arithmetic  1.4 us (2%)
    pallas_call x1, Pallas kernels, body(): pl.pallas_call(functools.partial(fused, nz, ny, nx), out_shape=jax.ShapeD...  65.2 us
    div x1, other arithmetic, body(): return (driver.astype(jnp.float32) + total) / denominator  1.4 us

profile of v1, /device:TPU:1, one launch (start us, length us, event | category | flops | bytes accessed | tf_op | source)
XLA Modules:
  0.0 66.6 jit_solution(3843661436894982739)
XLA Ops:
  0.0 0.0 copy-start.1
  0.0 0.0 copy-start.2
  0.0 0.0 copy-start
  0.0 65.2 %shard_map.73 = f32[32,128]{1,0:T(8,128)} custom-call(bf16[32,128]{1,0:T(8,128)(2,1)} %amp_ref.1, s32[1,32]{1,0:T(1,128)} %bitcast.5, bf16[32,6144]{1,0:T(8,128)(2,1)} %bitcast.4, bf16[64,12288]{1,0:T(8,128)(2,1)} %bitcast.3), custom_call_target="tpu_custom_call" | custom-call | tf_op jit(solution)/shard_map/pallas_call | solution.py:225
  65.2 0.0 copy-done.1
  65.2 0.0 copy-done.2
  65.2 0.0 copy-done
  65.2 1.4 %subtract_divide_fusion = f32[32,128]{1,0:T(8,128)} fusion(f32[32,128]{1,0:T(8,128)} %shard_map.73, bf16[32,128]{1,0:T(8,128)(2,1)S(1)} %copy-done, f32[128]{0:T(128)S(1)} %copy-done.1, f32[32]{0:T(128)S(1)} %copy-done.2), kind=kLoop, calls=%fused_computation | loop fusion | flops 16384 | bytes 41600 | tf_op jit(solution)/shard_map/div | solution.py:251
Async XLA Ops:
  0.0 65.2 %copy-start.1 = (f32[128]{0:T(128)S(1)}, f32[128]{0:T(128)}, u32[]{:S(2)}) copy-start(f32[128]{0:T(128)} %param.13) | copy-start | bytes 1540
  0.0 65.2 %copy-start.2 = (f32[32]{0:T(128)S(1)}, f32[32]{0:T(128)}, u32[]{:S(2)}) copy-start(f32[32]{0:T(128)} %param.12) | copy-start | bytes 388
  0.0 65.2 %copy-start = (bf16[32,128]{1,0:T(8,128)(2,1)S(1)}, bf16[32,128]{1,0:T(8,128)(2,1)}, u32[]{:S(2)}) copy-start(bf16[32,128]{1,0:T(8,128)(2,1)} %param.8) | copy-start | bytes 24580

commit v2 on v1

--- a/solution.py
+++ b/solution.py
@@ -12,13 +12,15 @@
 ROW_COL = ("row_0", "row_1", "row_2", "col")
 MESH = pl.DeviceIdType.MESH
 CORES = 2
+CHUNKS = 4
+AXIS = ("dy", "dz")
 
 
 def fused(
     nz, ny, nx, amp_ref, tgt_ref, ladder_hbm, cycle_hbm, out_ref,
     gath, ladder_v, cycle_v, placed, mix, ret,
     w_sem, ring_send, first_recv, second_recv, part_send, part_recv,
-    x_send, x_recv, back_send, back_recv,
+    a_send, t_send, x_recv, back_send, back_recv,
 ):
     z, y, core, x = (lax.axis_index(a) for a in ROW_COL)
     pair, occ = amp_ref.shape
@@ -38,10 +40,22 @@
         )
 
     barrier = pltpu.get_barrier_semaphore()
-    peers = [at(dz=1), at(dz=-1), at(dy=1), at(dy=-1), at(dc=1)]
-    peers += [at(dx=j) for j in range(1, nx)]
-    for peer in peers:
-        pl.semaphore_signal(barrier, inc=1, device_id=peer, device_id_type=MESH)
+
+    def greet(peers):
+        for peer in peers:
+            pl.semaphore_signal(barrier, inc=1, device_id=peer, device_id_type=MESH)
+
+    def peers_of(p):
+        n1 = ny if p == 0 else nz
+        along = [at(dx=j, **{AXIS[p]: o}) for o in range(n1) for j in range(nx) if o or j]
+        across = [at(**{AXIS[1 - p]: d}) for d in (1, -1)]
+        return along + across + [at(dc=1)]
+
+    for p in range(CORES):
+
+        @pl.when(core == p)
+        def _():
+            greet(peers_of(p))
 
     slot_ids = lax.broadcasted_iota(jnp.int32, (crow, pair), 0)
     onehot = (slot_ids == tgt_ref[...]).astype(jnp.float32).astype(jnp.bfloat16)
@@ -53,7 +67,11 @@
     my_part = pl.ds(pl.multiple_of(pair + x * cap, cap), cap)
     gath[core, my_slot, my_part, :] = placed[x]
 
-    pl.semaphore_wait(barrier, len(peers))
+    for p in range(CORES):
+
+        @pl.when(core == p)
+        def _():
+            pl.semaphore_wait(barrier, len(peers_of(p)))
 
     def remote(src, dst, send_sem, recv_sem, device):
         return pltpu.make_async_remote_copy(
@@ -61,27 +79,33 @@
             device_id=device, device_id_type=MESH,
         )
 
-    def out_x(j):
-        to = at(dx=j)
-        return remote(
-            placed.at[to[3]], gath.at[core, my_slot, my_part, :], x_send.at[j], x_recv.at[j], to
-        )
-
-    for j in range(1, nx):
-        out_x(j).start()
-    for j in range(1, nx):
-        out_x(j).wait_recv()
-
     partner = at(dc=1)
 
     def plane(p):
         n1, n2 = (ny, nz) if p == 0 else (nz, ny)
         i1, i2 = (y, z) if p == 0 else (z, y)
-        first = [at(dy=1), at(dy=-1)] if p == 0 else [at(dz=1), at(dz=-1)]
-        second = [at(dz=1), at(dz=-1)] if p == 0 else [at(dy=1), at(dy=-1)]
-
-        def block(a2, a1):
-            return gath.at[p, lax.rem(a2 + 2 * n2, n2) * n1 + lax.rem(a1 + 2 * n1, n1)]
+        second = [at(**{AXIS[1 - p]: d}) for d in (1, -1)]
+        size = n1 // CHUNKS
+        home = i1 // size
+        r2 = n2 // 2
+        across = [lax.rem(i2 + d + n2, n2) for d in range(-r2, r2 + 1)]
+        order = [lax.rem(home + (j + 1) // 2 * (1 if j % 2 else CHUNKS - 1), CHUNKS) for j in range(CHUNKS)]
+
+        hops = sorted(range(n1), key=lambda o: -min(o, n1 - o))
+        for o in hops:
+            for j in sorted(range(nx), key=lambda j: -min(j, nx - j)):
+                if o or j:
+                    to = at(dx=j, **{AXIS[p]: o})
+                    remote(
+                        placed.at[to[3]], gath.at[p, my_slot, my_part, :], t_send,
+                        first_recv.at[home] if o else x_recv, to,
+                    ).start()
+            if o:
+                mine = gath.at[p, my_slot, pl.ds(0, pair), :]
+                remote(mine, mine, a_send, first_recv.at[home], at(**{AXIS[p]: o})).start()
+
+        def chunk(d2, j, count=size):
+            return gath.at[p, pl.ds(across[r2 + d2] * n1 + order[j] * size, count)]
 
         def ring(src, recv_sem, device):
             return remote(src, src, ring_send, recv_sem, device)
@@ -89,61 +113,34 @@
         def to_partner(src):
             remote(src, src, part_send, part_recv, partner).start()
 
-        def launch(k, src):
+        for j in range(CHUNKS):
+            if j == 0:
+                rest = gath.at[p, my_slot, pl.ds(0, (nx - 1) * cap), :]
+                remote(rest, rest, t_send, x_recv, partner).wait_recv()
+            got = chunk(0, j, size if j else size - 1)
+            ring(got, first_recv.at[order[j]], partner).wait_recv()
+            src = chunk(0, j)
             for d in range(2):
-                ring(src, second_recv.at[d, k * (n2 // 2)], second[d]).start()
+                ring(src, second_recv.at[d, j * r2], second[d]).start()
             to_partner(src)
 
-        def step(t, carry):
-            def column(k, carry):
-                s1 = (k + 1) // 2
-                down = lax.rem(k + 1, 2)
-                j = jnp.where(down == 0, i1 - s1, i1 + s1)
-
-                @pl.when(t == s1)
-                def _():
-                    src = block(i2, j)
-                    for d in range(2):
-
-                        @pl.when((k > 0) & (down == d))
-                        def _():
-                            ring(src, first_recv.at[d, s1 - 1], first[d]).wait_recv()
-
-                            @pl.when(k + 2 < n1)
-                            def _():
-                                ring(src, first_recv.at[d, s1], first[d]).start()
-
-                    @pl.when(k == 0)
-                    def _():
-                        for d in range(2):
-                            ring(src, first_recv.at[d, 0], first[d]).start()
-
-                    launch(k, src)
-
-                s2 = t - s1
+        for s in range(1, r2 + 1):
+            for j in range(CHUNKS):
                 for d in range(2):
-                    if n2 % 2 == 0:
-                        last = jnp.where(down == d, n2 // 2, n2 // 2 - 1)
-                    else:
-                        last = n2 // 2
-
-                    @pl.when((s2 >= 1) & (s2 <= last))
-                    def _():
-                        src = block(i2 - s2 if d == 0 else i2 + s2, j)
-                        base = k * (n2 // 2)
-                        ring(src, second_recv.at[d, base + s2 - 1], second[d]).wait_recv()
-
-                        @pl.when(s2 < last)
-                        def _():
-                            ring(src, second_recv.at[d, base + s2], second[d]).start()
-
+                    last = r2 - (n2 % 2 == 0 and j % 2 != d)
+                    if s <= last:
+                        src = chunk(s if d else -s, j)
+                        ring(src, second_recv.at[d, j * r2 + s - 1], second[d]).wait_recv()
+                        if s < last:
+                            ring(src, second_recv.at[d, j * r2 + s], second[d]).start()
                         to_partner(src)
 
-                return carry
-
-            return lax.fori_loop(0, n1, column, carry)
-
-        lax.fori_loop(0, n1 // 2 + n2 // 2 + 1, step, 0)
+        sent = gath.at[p, pl.ds(0, n1 * (n2 - 1))]
+        ring(sent, x_recv, partner).wait_send()
+        a_all = gath.at[p, pl.ds(0, n1 - 1), pl.ds(0, pair), :]
+        remote(a_all, a_all, a_send, x_recv, partner).wait_send()
+        t_all = gath.at[p, pl.ds(0, n1 * nx - 1), pl.ds(0, cap), :]
+        remote(t_all, t_all, t_send, x_recv, partner).wait_send()
 
     for p in range(CORES):
         pl.when(core == p)(functools.partial(plane, p))
@@ -198,12 +195,9 @@
     for j in range(1, nx):
         back_x(j).start()
 
-    sent = gath.at[core, pl.ds(0, blocks - 1)]
-    remote(sent, sent, ring_send, first_recv.at[0, 0], partner).wait_send()
     mine = gath.at[core]
     remote(mine, mine, part_send, part_recv, partner).wait_send()
     for j in range(1, nx):
-        out_x(j).wait_send()
         back_x(j).wait_recv()
         back_x(j).wait_send()
     term = lax.dot_general(
@@ -218,7 +212,6 @@
     crow = cycle_kernel.shape[2]
     cap = crow // nx
     blocks = nz * ny
-    half = max((ny // 2) * nz, (nz // 2) * ny)
     vmem = pl.BlockSpec(memory_space=pltpu.VMEM)
     hbm = pl.BlockSpec(memory_space=pl.ANY)
     dma = pltpu.SemaphoreType.DMA
@@ -236,12 +229,13 @@
             pltpu.VMEM((nx, cap, occ), jnp.bfloat16),
             dma((2,)),
             dma,
-            dma((2, max(ny, nz) // 2)),
-            dma((2, half)),
-            dma,
-            dma,
-            dma((nx,)),
-            dma((nx,)),
+            dma((CHUNKS,)),
+            dma((2, CHUNKS * (max(ny, nz) // 2))),
+            dma,
+            dma,
+            dma,
+            dma,
+            dma,
             dma((nx,)),
             dma((nx,)),
         ],

time: 66.9 us -> 57.9 us (0.87)
  Pallas kernels: 65.2 us -> 56.2 us
    pallas_call x1, Pallas kernels: 65.2 us -> 56.2 us  [body(): pl.pallas_call(functools.partial(fused, nz, ny, nx), out_shape=jax.ShapeD...]
where the time goes in v2:
time: 57.9 us; the launch traced here: 57.6 us
  Pallas kernels  56.2 us (97%)
  other arithmetic  1.4 us (2%)
    pallas_call x1, Pallas kernels, body(): pl.pallas_call(functools.partial(fused, nz, ny, nx), out_shape=jax.ShapeD...  56.2 us
    div x1, other arithmetic, body(): return (driver.astype(jnp.float32) + total) / denominator  1.4 us

profile of v2, /device:TPU:1, one launch (start us, length us, event | category | flops | bytes accessed | tf_op | source)
XLA Modules:
  0.0 57.6 jit_solution(5741688617861533560)
XLA Ops:
  0.0 0.0 copy-start.1
  0.0 0.0 copy-start.2
  0.0 0.0 copy-start
  0.0 56.2 %shard_map.73 = f32[32,128]{1,0:T(8,128)} custom-call(bf16[32,128]{1,0:T(8,128)(2,1)} %amp_ref.1, s32[1,32]{1,0:T(1,128)} %bitcast.5, bf16[32,6144]{1,0:T(8,128)(2,1)} %bitcast.4, bf16[64,12288]{1,0:T(8,128)(2,1)} %bitcast.3), custom_call_target="tpu_custom_call" | custom-call | tf_op jit(solution)/shard_map/pallas_call | solution.py:218
  56.2 0.0 copy-done.1
  56.2 0.0 copy-done.2
  56.2 0.0 copy-done
  56.2 1.4 %subtract_divide_fusion = f32[32,128]{1,0:T(8,128)} fusion(f32[32,128]{1,0:T(8,128)} %shard_map.73, bf16[32,128]{1,0:T(8,128)(2,1)S(1)} %copy-done, f32[128]{0:T(128)S(1)} %copy-done.1, f32[32]{0:T(128)S(1)} %copy-done.2), kind=kLoop, calls=%fused_computation | loop fusion | flops 16384 | bytes 41600 | tf_op jit(solution)/shard_map/div | solution.py:245
Async XLA Ops:
  0.0 56.2 %copy-start.1 = (f32[128]{0:T(128)S(1)}, f32[128]{0:T(128)}, u32[]{:S(2)}) copy-start(f32[128]{0:T(128)} %param.13) | copy-start | bytes 1540
  0.0 56.2 %copy-start.2 = (f32[32]{0:T(128)S(1)}, f32[32]{0:T(128)}, u32[]{:S(2)}) copy-start(f32[32]{0:T(128)} %param.12) | copy-start | bytes 388
  0.0 56.2 %copy-start = (bf16[32,128]{1,0:T(8,128)(2,1)S(1)}, bf16[32,128]{1,0:T(8,128)(2,1)}, u32[]{:S(2)}) copy-start(bf16[32,128]{1,0:T(8,128)(2,1)} %param.8) | copy-start | bytes 24580

commit v3 on v1

v3 whole, which is shorter than its diff:
```python
import functools

import jax
import jax.numpy as jnp
from jax import lax
from jax.experimental import pallas as pl
from jax.experimental.pallas import tpu as pltpu
from jax.sharding import Mesh
from jax.sharding import PartitionSpec as P

ROW = ("row_0", "row_1", "row_2")
ROW_COL = ("row_0", "row_1", "row_2", "col")
MESH = pl.DeviceIdType.MESH
CORES = 2
CHUNKS = (4, 4)
SKIP = (2, 2)


def fused(
    nz, ny, nx, amp_ref, tgt_ref, ladder_hbm, cycle_hbm, out_ref,
    gath, ladder_v, cycle_v, placed, mix, ret,
    w_sem, first_send, first_recv, ring_send, ring_recv, part_send, part_recv,
    x_send, x_recv, back_send, back_recv,
):
    z, y, core, x = (lax.axis_index(a) for a in ROW_COL)
    pair, occ = amp_ref.shape
    cap = placed.shape[1]
    crow = nx * cap
    blocks = nz * ny
    half = (pair + crow) // 2
    here = (half - pair) // cap

    def at(dz=0, dy=0, dx=0, dc=0):
        return (
            lax.rem(z + dz + nz, nz), lax.rem(y + dy + ny, ny),
            lax.rem(core + dc, CORES), lax.rem(x + dx, nx),
        )

    barrier = pltpu.get_barrier_semaphore()
    peers = [at(dz=o) for o in range(1, nz)] + [at(dy=o) for o in range(1, ny)]
    peers += [at(dx=j) for j in range(1, nx)] + [at(dc=1)]
    for peer in peers:
        pl.semaphore_signal(barrier, inc=1, device_id=peer, device_id_type=MESH)
    load_l = pltpu.make_async_copy(ladder_hbm, ladder_v, w_sem.at[0])
    load_c = pltpu.make_async_copy(cycle_hbm, cycle_v, w_sem.at[1])
    load_l.start()
    load_c.start()

    slot_ids = lax.broadcasted_iota(jnp.int32, (crow, pair), 0)
    onehot = (slot_ids == tgt_ref[...]).astype(jnp.float32).astype(jnp.bfloat16)
    own = jnp.dot(onehot, amp_ref[...], preferred_element_type=jnp.float32)
    placed[...] = own.astype(jnp.bfloat16).reshape(nx, cap, occ)

    slots = [z * ny + y, y * nz + z]
    gath[0, core, slots[0], pl.ds(0, pair), :] = amp_ref[...]
    in_first = x < here
    my_half = jnp.where(in_first, 0, 1)
    my_slot = jnp.where(in_first, slots[0], slots[1])
    my_row = pl.multiple_of(jnp.where(in_first, pair + x * cap, (x - here) * cap), cap)
    gath[my_half, core, my_slot, pl.ds(my_row, cap), :] = placed[x]

    pl.semaphore_wait(barrier, len(peers))

    def remote(src, dst, send_sem, recv_sem, device):
        return pltpu.make_async_remote_copy(
            src_ref=src, dst_ref=dst, send_sem=send_sem, recv_sem=recv_sem,
            device_id=device, device_id_type=MESH,
        )

    def same(src, send_sem, recv_sem, device):
        return remote(src, src, send_sem, recv_sem, device)

    def out_x(j):
        to = at(dx=j)
        part = gath.at[my_half, core, my_slot, pl.ds(my_row, cap), :]
        return remote(placed.at[to[3]], part, x_send.at[j], x_recv.at[j], to)

    for j in range(1, nx):
        out_x(j).start()
    for j in range(1, nx):
        out_x(j).wait_recv()

    partner = at(dc=1)

    def plane(p):
        n1, n2 = (ny, nz) if p == 0 else (nz, ny)
        i1, i2 = (y, z) if p == 0 else (z, y)
        along, across = ("dy", "dz") if p == 0 else ("dz", "dy")
        second = [[at(**{across: d * k}) for k in (1, 2)] for d in (1, -1)]
        skip = SKIP[p]
        chunks = CHUNKS[p]
        size = n1 // chunks
        reach = n2 // 2
        home = i1 // size
        order = [
            lax.rem(home + (j + 1) // 2 * (1 if j % 2 else chunks - 1), chunks) for j in range(chunks)
        ]

        def chunk(d2, j, count=size):
            a2 = lax.rem(i2 + d2 + n2, n2)
            return gath.at[p, core, pl.ds(a2 * n1 + order[j] * size, count)]

        def hop(src, j, d, s, far=1):
            arrives = ring_recv.at[p, d, j * reach + s + far - 1]
            return same(src, ring_send.at[p], arrives, second[d][far - 1])

        def send_on(src, j, d, s):
            if s % skip == 0:
                for far in range(skip, 0, -1):
                    if s + far <= last(j, d):
                        hop(src, j, d, s, far).start()

        def last(j, d):
            return reach - (n2 % 2 == 0 and j % 2 != d)

        def to_partner(src):
            same(src, part_send, part_recv, partner).start()

        def begin():
            mine = gath.at[p, core, slots[p]]
            for o in sorted(range(1, n1), key=lambda o: -min(o, n1 - o)):
                same(mine, first_send.at[p], first_recv.at[p, home], at(**{along: o})).start()

        def launch():
            for j in range(chunks):
                if size > (j == 0):
                    got = chunk(0, j, size - (j == 0))
                    same(got, first_send.at[p], first_recv.at[p, order[j]], partner).wait_recv()
                src = chunk(0, j)
                for d in range(2):
                    send_on(src, j, d, 0)
                to_partner(src)

        def step(s):
            for j in range(chunks):
                for d in range(2):
                    if s <= last(j, d):
                        src = chunk(s if d else -s, j)
                        hop(src, j, d, s - 1).wait_recv()
                        send_on(src, j, d, s)
                        to_partner(src)

        def finish():
            sent = gath.at[p, core, pl.ds(0, n1 * (n2 - 1))]
            same(sent, ring_send.at[p], part_recv, partner).wait_send()
            sent = gath.at[p, core, pl.ds(0, n1 - 1)]
            same(sent, first_send.at[p], part_recv, partner).wait_send()

        return begin, launch, step, finish, reach

    planes = [plane(p) for p in range(2)]
    for p in (1, 0):
        planes[p][0]()
    for p in (0, 1):
        planes[p][1]()
    lists = [sorted(range(1, r[4] + 1), key=lambda s: (-(-s // k), s % k)) for r, k in zip(planes, SKIP)]
    for i in range(max(nz, ny) // 2):
        for p in (0, 1):
            if i < len(lists[p]):
                planes[p][2](lists[p][i])

    whole = gath.at[:, 1 - core]
    same(whole, part_send, part_recv, partner).wait_recv()
    load_l.wait()
    load_c.wait()

    def pieces(zz, y0, count, parts):
        rows = []
        for i in range(count):
            for c in range(CORES):
                for p, lo, n in parts:
                    slot = zz * ny + y0 + i if p == 0 else (y0 + i) * nz + zz
                    if n:
                        rows.append(gath[p, c, slot, pl.ds(lo, n), :])
        return jnp.concatenate(rows, axis=0)

    lad_parts = [(0, 0, pair)]
    cyc_parts = [(0, pair, half - pair), (1, 0, half)]
    lad_y = min(ny, 256 // (CORES * pair))
    cyc_y = min(ny, 256 // (CORES * crow))

    def contract(zz, carry):
        lad, cyc = carry
        for y0 in range(0, ny, lad_y):
            width = lad_y * CORES * pair
            start = pl.multiple_of((zz * ny + y0) * CORES * pair, width)
            lad += jnp.dot(
                ladder_v[:, pl.ds(start, width)], pieces(zz, y0, lad_y, lad_parts),
                preferred_element_type=jnp.float32,
            )
        for y0 in range(0, ny, cyc_y):
            width = cyc_y * CORES * crow
            start = pl.multiple_of((zz * ny + y0) * CORES * crow, width)
            cyc += jnp.dot(
                cycle_v[:, pl.ds(start, width)], pieces(zz, y0, cyc_y, cyc_parts),
                preferred_element_type=jnp.float32,
            )
        return lad, cyc

    lad, cyc = lax.fori_loop(
        0, nz, contract,
        (jnp.zeros((pair, occ), jnp.float32), jnp.zeros((crow, occ), jnp.float32)),
        unroll=3,
    )
    mix[...] = cyc.astype(jnp.bfloat16).reshape(nx, cap, occ)
    ret[x] = mix[x]

    def back_x(j):
        to = at(dx=j)
        return remote(mix.at[to[3]], ret.at[x], back_send.at[j], back_recv.at[j], to)

    for j in range(1, nx):
        back_x(j).start()
    for p in range(2):
        planes[p][3]()
    every = gath.at[:, core]
    same(every, part_send, part_recv, partner).wait_send()
    for j in range(1, nx):
        out_x(j).wait_send()
        back_x(j).wait_recv()
        back_x(j).wait_send()
    term = lax.dot_general(
        onehot, ret[...].reshape(crow, occ), (((0,), (0,)), ((), ())),
        preferred_element_type=jnp.float32,
    )
    out_ref[...] = lad + term


def body(nz, ny, nx, amplitudes, driver, ladder_integrals, cycle_kernel, cycle_target, vir_energy, occ_energy):
    pair, occ = amplitudes.shape
    crow = cycle_kernel.shape[2]
    cap = crow // nx
    blocks = nz * ny
    half = (pair + crow) // 2
    vmem = pl.BlockSpec(memory_space=pltpu.VMEM)
    hbm = pl.BlockSpec(memory_space=pl.ANY)
    dma = pltpu.SemaphoreType.DMA
    total = pl.pallas_call(
        functools.partial(fused, nz, ny, nx),
        out_shape=jax.ShapeDtypeStruct((pair, occ), jnp.float32),
        in_specs=[vmem, vmem, hbm, hbm],
        out_specs=vmem,
        scratch_shapes=[
            pltpu.VMEM((2, CORES, blocks, half, occ), jnp.bfloat16),
            pltpu.VMEM(ladder_integrals.shape[1:], jnp.bfloat16),
            pltpu.VMEM(cycle_kernel.shape[2:], jnp.bfloat16),
            pltpu.VMEM((nx, cap, occ), jnp.bfloat16),
            pltpu.VMEM((nx, cap, occ), jnp.bfloat16),
            pltpu.VMEM((nx, cap, occ), jnp.bfloat16),
            dma((2,)),
            dma((2,)),
            dma((2, max(CHUNKS))),
            dma((2,)),
            dma((2, 2, max(CHUNKS) * (max(ny, nz) // 2))),
            dma,
            dma,
            dma((nx,)),
            dma((nx,)),
            dma((nx,)),
            dma((nx,)),
        ],
        compiler_params=pltpu.CompilerParams(collective_id=0, has_side_effects=True),
    )(amplitudes, cycle_target.reshape(1, pair), ladder_integrals[0], cycle_kernel[0, 0])
    denominator = vir_energy[:, None] - occ_energy[None, :]
    return (driver.astype(jnp.float32) + total) / denominator


def solution(mesh, sizes=(12, 8)):
    nz, ny = sizes
    nx = mesh.shape["col"]
    finer = Mesh(mesh.devices.reshape(nz, ny, CORES, nx), ROW_COL)
    in_specs = (
        P(ROW_COL, None),
        P(ROW_COL, None),
        P("col", ROW, None),
        P(ROW, "col", None, None),
        P(ROW_COL),
        P(ROW_COL),
        P(),
    )
    return jax.shard_map(
        functools.partial(body, nz, ny, nx), mesh=finer, in_specs=in_specs,
        out_specs=P(ROW_COL, None), check_vma=False,
    )
```

time: 66.9 us -> 55.3 us (0.83)
  Pallas kernels: 65.2 us -> 53.6 us
    pallas_call x1, Pallas kernels: 65.2 us -> 53.6 us  [body(): pl.pallas_call(functools.partial(fused, nz, ny, nx), out_shape=jax.ShapeD...]
where the time goes in v3:
time: 55.3 us; the launch traced here: 55.1 us
  Pallas kernels  53.6 us (97%)
  other arithmetic  1.4 us (3%)
    pallas_call x1, Pallas kernels, body(): pl.pallas_call(functools.partial(fused, nz, ny, nx), out_shape=jax.ShapeD...  53.6 us
    div x1, other arithmetic, body(): return (driver.astype(jnp.float32) + total) / denominator  1.4 us

profile of v3, /device:TPU:1, one launch (start us, length us, event | category | flops | bytes accessed | tf_op | source)
XLA Modules:
  0.0 55.1 jit_solution(2126504664864402451)
XLA Ops:
  0.0 0.0 copy-start.1
  0.0 0.0 copy-start.2
  0.0 0.0 copy-start
  0.0 53.6 %shard_map.73 = f32[32,128]{1,0:T(8,128)} custom-call(bf16[32,128]{1,0:T(8,128)(2,1)} %amp_ref.1, s32[1,32]{1,0:T(1,128)} %bitcast.5, bf16[32,6144]{1,0:T(8,128)(2,1)} %bitcast.4, bf16[64,12288]{1,0:T(8,128)(2,1)} %bitcast.3), custom_call_target="tpu_custom_call" | custom-call | tf_op jit(solution)/shard_map/pallas_call | solution.py:238
  53.6 0.0 copy-done.1
  53.6 0.0 copy-done.2
  53.6 0.0 copy-done
  53.7 1.4 %subtract_divide_fusion = f32[32,128]{1,0:T(8,128)} fusion(f32[32,128]{1,0:T(8,128)} %shard_map.73, bf16[32,128]{1,0:T(8,128)(2,1)S(1)} %copy-done, f32[128]{0:T(128)S(1)} %copy-done.1, f32[32]{0:T(128)S(1)} %copy-done.2), kind=kLoop, calls=%fused_computation | loop fusion | flops 16384 | bytes 41600 | tf_op jit(solution)/shard_map/div | solution.py:265
Async XLA Ops:
  0.0 53.6 %copy-start.1 = (f32[128]{0:T(128)S(1)}, f32[128]{0:T(128)}, u32[]{:S(2)}) copy-start(f32[128]{0:T(128)} %param.13) | copy-start | bytes 1540
  0.0 53.6 %copy-start.2 = (f32[32]{0:T(128)S(1)}, f32[32]{0:T(128)}, u32[]{:S(2)}) copy-start(f32[32]{0:T(128)} %param.12) | copy-start | bytes 388
  0.0 53.6 %copy-start = (bf16[32,128]{1,0:T(8,128)(2,1)S(1)}, bf16[32,128]{1,0:T(8,128)(2,1)}, u32[]{:S(2)}) copy-start(bf16[32,128]{1,0:T(8,128)(2,1)} %param.8) | copy-start | bytes 24580

commit v4 on v3

--- a/solution.py
+++ b/solution.py
@@ -179,8 +179,7 @@
     lad_y = min(ny, 256 // (CORES * pair))
     cyc_y = min(ny, 256 // (CORES * crow))
 
-    def contract(zz, carry):
-        lad, cyc = carry
+    def ladder_sum(zz, lad):
         for y0 in range(0, ny, lad_y):
             width = lad_y * CORES * pair
             start = pl.multiple_of((zz * ny + y0) * CORES * pair, width)
@@ -188,6 +187,9 @@
                 ladder_v[:, pl.ds(start, width)], pieces(zz, y0, lad_y, lad_parts),
                 preferred_element_type=jnp.float32,
             )
+        return lad
+
+    def cycle_sum(zz, cyc):
         for y0 in range(0, ny, cyc_y):
             width = cyc_y * CORES * crow
             start = pl.multiple_of((zz * ny + y0) * CORES * crow, width)
@@ -195,13 +197,9 @@
                 cycle_v[:, pl.ds(start, width)], pieces(zz, y0, cyc_y, cyc_parts),
                 preferred_element_type=jnp.float32,
             )
-        return lad, cyc
-
-    lad, cyc = lax.fori_loop(
-        0, nz, contract,
-        (jnp.zeros((pair, occ), jnp.float32), jnp.zeros((crow, occ), jnp.float32)),
-        unroll=3,
-    )
+        return cyc
+
+    cyc = lax.fori_loop(0, nz, cycle_sum, jnp.zeros((crow, occ), jnp.float32), unroll=3)
     mix[...] = cyc.astype(jnp.bfloat16).reshape(nx, cap, occ)
     ret[x] = mix[x]
 
@@ -211,6 +209,7 @@
 
     for j in range(1, nx):
         back_x(j).start()
+    lad = lax.fori_loop(0, nz, ladder_sum, jnp.zeros((pair, occ), jnp.float32), unroll=3)
     for p in range(2):
         planes[p][3]()
     every = gath.at[:, core]

time: 55.3 us -> 55 us (level)
  no operation moved by 1% of the time
where the time goes in v4:
time: 55 us; the launch traced here: 54.7 us
  Pallas kernels  53.3 us (97%)
  other arithmetic  1.4 us (3%)
    pallas_call x1, Pallas kernels, body(): pl.pallas_call(functools.partial(fused, nz, ny, nx), out_shape=jax.ShapeD...  53.3 us
    div x1, other arithmetic, body(): return (driver.astype(jnp.float32) + total) / denominator  1.4 us

profile of v4, /device:TPU:1, one launch (start us, length us, event | category | flops | bytes accessed | tf_op | source)
XLA Modules:
  0.0 54.7 jit_solution(14590815844358035382)
XLA Ops:
  0.0 0.0 copy-start.1
  0.0 0.0 copy-start.2
  0.0 0.0 copy-start
  0.0 53.3 %shard_map.73 = f32[32,128]{1,0:T(8,128)} custom-call(bf16[32,128]{1,0:T(8,128)(2,1)} %amp_ref.1, s32[1,32]{1,0:T(1,128)} %bitcast.5, bf16[32,6144]{1,0:T(8,128)(2,1)} %bitcast.4, bf16[64,12288]{1,0:T(8,128)(2,1)} %bitcast.3), custom_call_target="tpu_custom_call" | custom-call | tf_op jit(solution)/shard_map/pallas_call | solution.py:237
  53.3 0.0 copy-done.1
  53.3 0.0 copy-done.2
  53.3 0.0 copy-done
  53.3 1.4 %subtract_divide_fusion = f32[32,128]{1,0:T(8,128)} fusion(f32[32,128]{1,0:T(8,128)} %shard_map.73, bf16[32,128]{1,0:T(8,128)(2,1)S(1)} %copy-done, f32[128]{0:T(128)S(1)} %copy-done.1, f32[32]{0:T(128)S(1)} %copy-done.2), kind=kLoop, calls=%fused_computation | loop fusion | flops 16384 | bytes 41600 | tf_op jit(solution)/shard_map/div | solution.py:264
Async XLA Ops:
  0.0 53.3 %copy-start.1 = (f32[128]{0:T(128)S(1)}, f32[128]{0:T(128)}, u32[]{:S(2)}) copy-start(f32[128]{0:T(128)} %param.13) | copy-start | bytes 1540
  0.0 53.3 %copy-start.2 = (f32[32]{0:T(128)S(1)}, f32[32]{0:T(128)}, u32[]{:S(2)}) copy-start(f32[32]{0:T(128)} %param.12) | copy-start | bytes 388
  0.0 53.3 %copy-start = (bf16[32,128]{1,0:T(8,128)(2,1)S(1)}, bf16[32,128]{1,0:T(8,128)(2,1)}, u32[]{:S(2)}) copy-start(bf16[32,128]{1,0:T(8,128)(2,1)} %param.8) | copy-start | bytes 24580
